TPU v7x, 32 devices: a whole 2x2x4 slice. The times are simulated.
32 devices in a mesh: seq: 16 (over z, y, core), dp: 2 (over x).
Axes of the slice: x: 2, y: 2, z: 4, core: 2. Of those that a mesh axis runs over, the one named last changes fastest.
Arguments:
- queries: bfloat16 [2, 4096, 2048], P('dp', 'seq'), may hold values from -6 to 6
- key_rows: bfloat16 [2, 4096, 2048], P('dp', 'seq'), may hold values from -6 to 6
- value_rows: bfloat16 [2, 4096, 2048], P('dp', 'seq'), may hold values from -6 to 6
- out_grad: bfloat16 [2, 4096, 2048], P('dp', 'seq'), may hold values from -6 to 6
- out_weight: bfloat16 [2048, 2048], P('seq', 'dp'), may hold values from -0.125 to 0.125
Outputs:
- query_grad: bfloat16 [2, 4096, 2048], P('dp', 'seq')
- key_grad: bfloat16 [2, 4096, 2048], P('dp', 'seq')
- value_grad: bfloat16 [2, 4096, 2048], P('dp', 'seq')
- weight_grad: float32 [2048, 2048], P('seq', 'dp')
All inputs are finite; a program needn't handle non-finite values.
Results may differ from a plain program's by a relative error of at most 0.014.
Values may be sent and summed in bfloat16 or wider, within the bound.
A program may use at most 192 MiB of HBM per device.

v0:
```python
import math
import jax
import jax.numpy as jnp
from jax import lax
from jax.sharding import PartitionSpec as P

HEADS = 16
HEAD = 128
HD = 2048


def prefix_2(part, axis, combine, identity, reverse):
    count = lax.axis_size(axis)
    place = lax.axis_index(axis)
    ahead = count - 1 - place if reverse else place
    gathered = lax.all_gather(part, axis)
    state = jnp.zeros_like(part) + jnp.asarray(identity, part.dtype)

    def one(step, state):
        source = count - 1 - step if reverse else step
        return combine(state, lax.dynamic_index_in_dim(gathered, source, 0, False))

    return lax.fori_loop(0, ahead, one, state)


def add_sums(earlier, later):
    return earlier + later


def shards(queries, key_rows, value_rows, out_grad, out_weight):
    tokens_dev = queries.shape[1]
    seq_devices = lax.axis_size("seq")
    data_devices = lax.axis_size("dp")
    seq_length = tokens_dev * seq_devices
    seq_count = queries.shape[0] * data_devices
    score_scale = 1.0 / math.sqrt(HEAD * seq_length)
    grad_scale = 1.0 / math.sqrt(seq_count * seq_length)
    query_flat = queries[0]
    grad_flat = out_grad[0]
    query_h = query_flat.reshape(tokens_dev, HEADS, HEAD)
    key_h = key_rows[0].reshape(tokens_dev, HEADS, HEAD)
    value_h = value_rows[0].reshape(tokens_dev, HEADS, HEAD)
    row_ids = lax.broadcasted_iota(jnp.int32, (tokens_dev, tokens_dev), 0)
    col_ids = lax.broadcasted_iota(jnp.int32, (tokens_dev, tokens_dev), 1)
    causal = (row_ids >= col_ids).astype(jnp.float32)
    empty_state = jnp.zeros((HEADS, HEAD, HEAD), jnp.float32)
    kv_local = jnp.einsum("shd,she->hde", key_h, value_h, preferred_element_type=jnp.float32)
    wide_weight = lax.all_gather(out_weight, "dp", axis=1, tiled=True)
    head_grad = lax.dot_general(
        grad_flat,
        lax.all_gather(wide_weight, "seq", axis=0, tiled=True),
        (((1,), (1,)), ((), ())),
        preferred_element_type=jnp.float32,
    ).astype(jnp.bfloat16)
    grad_h = head_grad.reshape(tokens_dev, HEADS, HEAD)
    query_dout = jnp.einsum("thd,the->hde", query_h, grad_h, preferred_element_type=jnp.float32)
    prefix = prefix_2(kv_local, "seq", add_sums, empty_state, False)
    suffix = prefix_2(query_dout, "seq", add_sums, empty_state, True)
    prefix_scaled = (score_scale * prefix).astype(jnp.bfloat16)
    suffix_scaled = (score_scale * suffix).astype(jnp.bfloat16)
    scores = (
        score_scale
        * jnp.einsum("thd,shd->hts", query_h, key_h, preferred_element_type=jnp.float32)
        * causal
    ).astype(jnp.bfloat16)
    attended = jnp.einsum("hts,shd->thd", scores, value_h, preferred_element_type=jnp.float32)
    attended = attended + jnp.einsum(
        "thd,hde->the", query_h, prefix_scaled, preferred_element_type=jnp.float32
    )
    attended = attended.astype(jnp.bfloat16).reshape(tokens_dev, HD)
    row_sums = lax.psum_scatter(
        (
            grad_scale
            * lax.dot_general(
                attended, grad_flat, (((0,), (0,)), ((), ())), preferred_element_type=jnp.float32
            )
        ).astype(jnp.bfloat16),
        "seq",
        scatter_dimension=0,
        tiled=True,
    )
    weight_grad = lax.psum_scatter(row_sums, "dp", scatter_dimension=1, tiled=True).astype(
        jnp.float32
    )
    grad_scores = (
        score_scale
        * jnp.einsum("the,she->hts", grad_h, value_h, preferred_element_type=jnp.float32)
        * causal
    ).astype(jnp.bfloat16)
    query_g = jnp.einsum("hts,shd->thd", grad_scores, key_h, preferred_element_type=jnp.float32)
    query_g = query_g + jnp.einsum(
        "the,hde->thd", grad_h, prefix_scaled, preferred_element_type=jnp.float32
    )
    key_g = jnp.einsum("hts,thd->shd", grad_scores, query_h, preferred_element_type=jnp.float32)
    key_g = key_g + jnp.einsum(
        "she,hde->shd", value_h, suffix_scaled, preferred_element_type=jnp.float32
    )
    value_g = jnp.einsum("hts,the->she", scores, grad_h, preferred_element_type=jnp.float32)
    value_g = value_g + jnp.einsum(
        "shd,hde->she", key_h, suffix_scaled, preferred_element_type=jnp.float32
    )
    query_grad = query_g.astype(jnp.bfloat16).reshape(1, tokens_dev, HD)
    key_grad = key_g.astype(jnp.bfloat16).reshape(1, tokens_dev, HD)
    value_grad = value_g.astype(jnp.bfloat16).reshape(1, tokens_dev, HD)
    return (query_grad, key_grad, value_grad, weight_grad)


def solution(mesh):
    return jax.shard_map(
        shards,
        mesh=mesh,
        in_specs=(
            P("dp", "seq", None),
            P("dp", "seq", None),
            P("dp", "seq", None),
            P("dp", "seq", None),
            P("seq", "dp"),
        ),
        out_specs=(
            P("dp", "seq", None),
            P("dp", "seq", None),
            P("dp", "seq", None),
            P("seq", "dp"),
        ),
        check_vma=False,
    )
```

profile of v0, /device:TPU:0, one launch (start us, length us, event | category | flops | bytes accessed | tf_op | source)
XLA Modules:
  0.0 536.6 jit_solution(13903750123057285457)
XLA Ops:
  7.2 1.6 copy.56
  8.8 1.8 copy.57
  16.0 2.2 fusion.22
  18.2 123.7 %all-gather.8.cloned.1.call-done = f32[256,128,128]{2,1,0:T(8,128)} async-done(((f32[16,128,128]{2,1,0:T(8,128)}), f32[256,128,128]{2,1,0:T(8,128)}) %all-gather.8.cloned.1.call-update) | async-done | bytes 16777232 | tf_op jit(solution)/shard_map/all_gather | solution.py:16
  142.0 2.5 fusion
  144.5 5.7 %multiply_convert_fusion = bf16[2048,2048]{1,0:T(8,128)(2,1)} fusion(bf16[256,2048]{0,1:T(8,128)(2,1)S(1)} %bitcast.84, bf16[1,256,2048]{2,1,0:T(8,128)(2,1)S(1)} %copy-done), kind=kOutput, calls=%fused_computation.2 | convolution fusion | flops 2155872256 | bytes 10485760 | tf_op jit(solution)/shard_map/dot_general | solution.py:74
  150.2 10.2 %all_gather.18 = bf16[128,2048]{1,0:T(8,128)(2,1)} all-gather(bf16[128,1024]{1,0:T(8,128)(2,1)} %param.13), channel_id=1, replica_groups=mesh['seq'=16,'dp'=2] {'dp'}, dimensions={1}, use_global_device_ids=true | all-gather | bytes 786432 | tf_op jit(solution)/shard_map/all_gather | solution.py:48
  160.5 115.1 %reduce-scatter.3.cloned.1.call-done = bf16[128,2048]{1,0:T(8,128)(2,1)} async-done(((bf16[2048,2048]{1,0:T(8,128)(2,1)}), bf16[128,2048]{1,0:T(8,128)(2,1)}) %reduce-scatter.3.cloned.1.call-update) | async-done | bytes 524304 | tf_op jit(solution)/shard_map/reduce_scatter | solution.py:71
  275.9 76.6 %all-gather.6.cloned.1.call-done = bf16[2048,2048]{1,0:T(8,128)(2,1)} async-done(((bf16[128,2048]{1,0:T(8,128)(2,1)}), bf16[2048,2048]{1,0:T(8,128)(2,1)}) %all-gather.6.cloned.1.call-update) | async-done | bytes 8388624 | tf_op jit(solution)/shard_map/all_gather | solution.py:51
  352.5 6.8 %convolution_convert_fusion = bf16[256,2048]{1,0:T(8,128)(2,1)} fusion(bf16[2048,2048]{1,0:T(8,128)(2,1)} %all-gather.6.cloned.1.call-done, bf16[1,256,2048]{2,1,0:T(8,128)(2,1)S(1)} %copy-done), kind=kOutput, calls=%fused_computation.5 | convolution fusion | flops 2148007936 | bytes 10485760 | tf_op jit(solution)/shard_map/dot_general | solution.py:49
  359.2 2.3 copy.55
  361.6 2.7 convolution_bitcast_fusion
  364.2 2.7 copy.40
  366.9 2.0 multiply_convert_fusion.2
  370.2 1.9 fusion.11
  372.9 1.8 fusion.21
  376.1 2.3 copy.50
  378.4 1.8 convert_element_type.52
  380.2 116.4 %all-gather.10.cloned.1.call-done = f32[256,128,128]{2,1,0:T(8,128)} async-done(((f32[16,128,128]{2,1,0:T(8,128)}), f32[256,128,128]{2,1,0:T(8,128)}) %all-gather.10.cloned.1.call-update) | async-done | bytes 16777232 | tf_op jit(solution)/shard_map/all_gather | solution.py:16
  496.7 22.7 %while.23 = (s32[]{:T(128)}, f32[16,128,128]{2,1,0:T(8,128)S(1)}, s32[]{:T(128)}, f32[16,16,128,128]{3,2,1,0:T(8,128)}, s32[]{:T(128)}, /*index=5*/s32[]{:T(128)}, s32[]{:T(128)}, s32[]{:T(128)}) while((s32[]{:T(128)}, f32[16,128,128]{2,1,0:T(8,128)S(1)}, s32[]{:T(128)}, f32[16,16,128,128]{3,2,1,0:T(8,128)}, s32[]{:T(128)}, ...), condition=%wide.region_3.4_spmd, body=%wide.region_2.3_spmd.sunk | while | flops 262150 | bytes 3145871 | solution.py:23
  519.3 3.0 fusion.1
  522.3 2.3 copy.51
  524.6 3.2 add_convert_fusion
  527.8 2.3 copy.52
  (55 shorter events, 31.7 us)
Async XLA Ops:
  7.2 137.3 %copy-start = (bf16[1,256,2048]{2,1,0:T(8,128)(2,1)S(1)}, bf16[1,256,2048]{2,1,0:T(8,128)(2,1)}, u32[]{:S(2)}) copy-start(bf16[1,256,2048]{2,1,0:T(8,128)(2,1)} %param.12) | copy-start | bytes 3145732
  7.2 134.7 %all-gather.8.cloned.1.call-start = ((), (), s32[]{:S(2)}) async-start(), calls=%async_computation.5 | async-start | bytes 17825792 | tf_op jit(solution)/shard_map/all_gather | solution.py:16
  8.8 5.6 %copy-start.2 = (bf16[1,256,2048]{1,2,0:T(8,128)(2,1)}, bf16[1,256,2048]{1,2,0:T(8,128)(2,1)S(1)}, u32[]{:S(2)}) copy-start(bf16[1,256,2048]{1,2,0:T(8,128)(2,1)S(1)} %copy.56) | copy-start | bytes 3145732
  12.1 263.5 %reduce-scatter.3.cloned.1.call-start = ((), (), s32[]{:S(2)}) async-start(), calls=%async_computation.3 | async-start | bytes 8912896 | tf_op jit(solution)/shard_map/reduce_scatter | solution.py:71
  13.6 1.0 copy-start.4
  14.6 1.3 copy-start.8
  150.2 202.3 %all-gather.6.cloned.1.call-start = ((), (), s32[]{:S(2)}) async-start(), calls=%async_computation.2 | async-start | bytes 8912896 | tf_op jit(solution)/shard_map/all_gather | solution.py:51
  160.5 217.9 %reduce-scatter.5.cloned.1.call-start = ((), (), s32[]{:S(2)}) async-start(), calls=%async_computation.4 | async-start | bytes 786432 | tf_op jit(solution)/shard_map/reduce_scatter | solution.py:82
  275.6 220.9 %all-gather.10.cloned.1.call-start = ((), (), s32[]{:S(2)}) async-start(), calls=%async_computation.6 | async-start | bytes 17825792 | tf_op jit(solution)/shard_map/all_gather | solution.py:16
  359.2 2.4 copy-start.5
  364.2 2.7 copy-start.3
  368.9 1.2 copy-start.6
  370.2 1.9 copy-start.7
  370.2 2.7 copy-start.9
  524.6 5.5 %copy-start.1 = (bf16[1,256,2048]{2,1,0:T(8,128)(2,1)S(1)}, bf16[1,256,2048]{2,1,0:T(8,128)(2,1)}, u32[]{:S(2)}) copy-start(bf16[1,256,2048]{2,1,0:T(8,128)(2,1)} %param.12) | copy-start | bytes 3145732
Sparse Core Ops, SparseCore 0:
  12.2 129.5 all-gather.7
  150.3 125.2 reduce-scatter.2
  277.8 74.6 all-gather.5
  354.6 12.7 reduce-scatter.4
  369.6 126.8 all-gather.9
where the time goes:
time: 538 us; the launch traced here: 537 us
  waiting for transfers between devices  432 us (80%)
  matrix products  36 us (7%)
  other arithmetic  24.1 us (4%)
  local copies, waits for them, and re-layouts  19.7 us (4%)
  between operations  13.9 us (3%)
  blocking collectives  10.2 us (2%)
    all_gather x2, waiting for transfers between devices, prefix_2(): gathered = lax.all_gather(part, axis)  240 us
    reduce_scatter x1, waiting for transfers between devices, shards(): lax.psum_scatter((grad_scale * lax.dot_general(attended, grad_flat, (((0,...  115 us
    all_gather x1, waiting for transfers between devices, shards(): lax.all_gather(wide_weight, 'seq', axis=0, tiled=True)  76.6 us
    add x15, other arithmetic, add_sums(): return earlier + later  22.3 us
    unnamed x25, local copies, waits for them, and re-layouts  12.9 us
  transfers between devices with their start and end apart: 5, of which 4 were waited for; matrix products, arithmetic and copies ran while one was open for 6% of the time, Pallas kernels for 0%

commit v1 on v0

--- a/solution.py
+++ b/solution.py
@@ -7,6 +7,36 @@
 HEADS = 16
 HEAD = 128
 HD = 2048
+
+
+def shifts_all_plan(message, comm_axis="seq"):
+    right_arr, v_now, everything = (
+        jax.lax.psum(1, comm_axis),
+        jax.lax.axis_index(comm_axis),
+        message.shape[0],
+    )
+    pool = [at * right_arr if no == 0 else at for no, at in enumerate(message.shape)]
+    local_now = lax.dynamic_update_slice_in_dim(
+        jnp.zeros(pool, message.dtype), message, v_now * everything, axis=0
+    )
+    main = tall = message
+    src_i = 1
+    while src_i < right_arr // 2 + 1:
+        main = jax.lax.ppermute(
+            main, comm_axis, [(no, (no + 1) % right_arr) for no in range(right_arr)]
+        )
+        local_now = lax.dynamic_update_slice_in_dim(
+            local_now, main, (v_now - src_i) % right_arr * everything, axis=0
+        )
+        if 2 * src_i < right_arr:
+            tall = jax.lax.ppermute(
+                tall, comm_axis, [(no, (no - 1) % right_arr) for no in range(right_arr)]
+            )
+            local_now = lax.dynamic_update_slice_in_dim(
+                local_now, tall, (v_now + src_i) % right_arr * everything, axis=0
+            )
+        src_i += 1
+    return local_now
 
 
 def prefix_2(part, axis, combine, identity, reverse):
@@ -48,7 +78,7 @@
     wide_weight = lax.all_gather(out_weight, "dp", axis=1, tiled=True)
     head_grad = lax.dot_general(
         grad_flat,
-        lax.all_gather(wide_weight, "seq", axis=0, tiled=True),
+        shifts_all_plan(wide_weight),
         (((1,), (1,)), ((), ())),
         preferred_element_type=jnp.float32,
     ).astype(jnp.bfloat16)

time: 538 us -> 494 us (0.918)
  waiting for transfers between devices: 432 us -> 305 us
  starting transfers between devices: 0.38 us -> 61.6 us
  local copies, waits for them, and re-layouts: 19.7 us -> 43.9 us
    reduce_scatter x1, waiting for transfers between devices: 115 us -> 0.01 us  [shards(): lax.psum_scatter((grad_scale * lax.dot_general(attended, grad_flat, (((0,...]
    all_gather x1 -> x0, waiting for transfers between devices: 76.6 us -> none  [shards(): lax.all_gather(wide_weight, 'seq', axis=0, tiled=True)]
    ppermute x0 -> x15, waiting for transfers between devices: none -> 67.4 us  [the longest x8 55.6 us: shifts_all_plan(): jax.lax.ppermute(main, comm_axis, [(no, (no + 1) % right_arr) for no in r...]
    ppermute x0 -> x15, starting transfers between devices: none -> 61.5 us  [the longest x7 60.9 us: shifts_all_plan(): jax.lax.ppermute(tall, comm_axis, [(no, (no - 1) % right_arr) for no in r...]
    dynamic_update_slice x0 -> x16, local copies, waits for them, and re-layouts: none -> 20.8 us  [the longest x8 11 us: shifts_all_plan(): lax.dynamic_update_slice_in_dim(local_now, main, (v_now - src_i) % right_...]
    unnamed x25 -> x31, local copies, waits for them, and re-layouts: 12.9 us -> 14.4 us
  transfers between devices with their start and end apart: 5 -> 19, of which waited for: 4 -> 14; matrix products, arithmetic and copies ran while one was open for 6% -> 17% of each run, Pallas kernels for 0% -> 0%
where the time goes in v1:
time: 494 us; the launch traced here: 492 us
  waiting for transfers between devices  305 us (62%)
  starting transfers between devices  61.6 us (12%)
  local copies, waits for them, and re-layouts  43.9 us (9%)
  matrix products  34.6 us (7%)
  other arithmetic  24.1 us (5%)
  between operations  14 us (3%)
  blocking collectives  9.31 us (2%)
    all_gather x2, waiting for transfers between devices, prefix_2(): gathered = lax.all_gather(part, axis)  237 us
    ppermute x7, starting transfers between devices, shifts_all_plan(): jax.lax.ppermute(tall, comm_axis, [(no, (no - 1) % right_arr) for no in r...  60.9 us
    ppermute x8, waiting for transfers between devices, shifts_all_plan(): jax.lax.ppermute(main, comm_axis, [(no, (no + 1) % right_arr) for no in r...  55.6 us
    add x15, other arithmetic, add_sums(): return earlier + later  22.3 us
    unnamed x31, local copies, waits for them, and re-layouts  14.4 us
    ppermute x7, waiting for transfers between devices, shifts_all_plan(): jax.lax.ppermute(tall, comm_axis, [(no, (no - 1) % right_arr) for no in r...  11.8 us
    dynamic_update_slice x8, local copies, waits for them, and re-layouts, shifts_all_plan(): lax.dynamic_update_slice_in_dim(local_now, main, (v_now - src_i) % right_...  11 us
  transfers between devices with their start and end apart: 19, of which 14 were waited for; matrix products, arithmetic and copies ran while one was open for 17% of the time, Pallas kernels for 0%

profile of v1, /device:TPU:0, one launch (start us, length us, event | category | flops | bytes accessed | tf_op | source)
XLA Modules:
  0.0 492.4 jit_solution(18183826916400708576)
XLA Ops:
  18.9 123.0 %all-gather.5.cloned.1.call-done = f32[256,128,128]{2,1,0:T(8,128)} async-done(((f32[16,128,128]{2,1,0:T(8,128)}), f32[256,128,128]{2,1,0:T(8,128)}) %all-gather.5.cloned.1.call-update) | async-done | bytes 16777232 | tf_op jit(solution)/shard_map/all_gather | solution.py:46
  144.5 5.6 %multiply_convert_fusion = bf16[2048,2048]{1,0:T(8,128)(2,1)} fusion(bf16[256,2048]{0,1:T(8,128)(2,1)S(1)} %bitcast.86, bf16[1,256,2048]{2,1,0:T(8,128)(2,1)S(1)} %copy-done), kind=kOutput, calls=%fused_computation.2 | convolution fusion | flops 2155872256 | bytes 10485760 | tf_op jit(solution)/shard_map/dot_general | solution.py:104
  150.2 9.3 %all_gather.15 = bf16[128,2048]{1,0:T(8,128)(2,1)S(1)} all-gather(bf16[128,1024]{1,0:T(8,128)(2,1)} %param.13), channel_id=1, replica_groups=mesh['seq'=16,'dp'=2] {'dp'}, dimensions={1}, use_global_device_ids=true | all-gather | bytes 786432 | tf_op jit(solution)/shard_map/all_gather | solution.py:78
  160.3 22.6 %collective-permute-start.1 = (bf16[128,2048]{1,0:T(8,128)(2,1)S(1)}, bf16[128,2048]{1,0:T(8,128)(2,1)S(1)}, u32[]{:S(2)}, u32[]{:S(2)}) collective-permute-start(bf16[128,2048]{1,0:T(8,128)(2,1)S(1)} %all_gather.15), channel_id=1, source_target_pairs={{0,30},{2,0},{4,2},{6,4},{8,6},{10,8},{12,10},{14,12},{16,14},{18,... | collective-permute-start | bytes 1572872 | tf_op jit(solution)/shard_map/ppermute | solution.py:32
  182.9 6.2 %collective-permute-done = bf16[128,2048]{1,0:T(8,128)(2,1)S(1)} collective-permute-done((bf16[128,2048]{1,0:T(8,128)(2,1)S(1)}, bf16[128,2048]{1,0:T(8,128)(2,1)S(1)}, u32[]{:S(2)}, u32[]{:S(2)}) %collective-permute-start) | collective-permute-done | bytes 524320 | tf_op jit(solution)/shard_map/ppermute | solution.py:25
  190.4 4.7 collective-permute-start.3
  195.1 5.5 %collective-permute-done.2 = bf16[128,2048]{1,0:T(8,128)(2,1)} collective-permute-done((bf16[128,2048]{1,0:T(8,128)(2,1)S(1)}, bf16[128,2048]{1,0:T(8,128)(2,1)}, u32[]{:S(2)}, u32[]{:S(2)}) %collective-permute-start.2) | collective-permute-done | bytes 524320 | tf_op jit(solution)/shard_map/ppermute | solution.py:25
  201.8 4.8 collective-permute-start.5
  206.6 14.4 %collective-permute-done.4 = bf16[128,2048]{1,0:T(8,128)(2,1)} collective-permute-done((bf16[128,2048]{1,0:T(8,128)(2,1)}, bf16[128,2048]{1,0:T(8,128)(2,1)}, u32[]{:S(2)}, u32[]{:S(2)}) %collective-permute-start.4) | collective-permute-done | bytes 524320 | tf_op jit(solution)/shard_map/ppermute | solution.py:25
  221.1 4.3 broadcast_in_dim.8
  228.2 4.9 collective-permute-start.7
  235.0 9.5 %collective-permute-done.6 = bf16[128,2048]{1,0:T(8,128)(2,1)} collective-permute-done((bf16[128,2048]{1,0:T(8,128)(2,1)}, bf16[128,2048]{1,0:T(8,128)(2,1)}, u32[]{:S(2)}, u32[]{:S(2)}) %collective-permute-start.6) | collective-permute-done | bytes 524320 | tf_op jit(solution)/shard_map/ppermute | solution.py:25
  248.3 4.4 collective-permute-start.9
  254.6 2.8 collective-permute-done.8
  261.2 14.7 %collective-permute-start.11 = (bf16[128,2048]{1,0:T(8,128)(2,1)S(1)}, bf16[128,2048]{1,0:T(8,128)(2,1)S(1)}, u32[]{:S(2)}, u32[]{:S(2)}) collective-permute-start(bf16[128,2048]{1,0:T(8,128)(2,1)S(1)} %collective-permute-done.9), channel_id=1, source_target_pairs={{0,30},{2,0},{4,2},{6,4},{8,6},{10,8},{12,10},{14,12},{16,14},{18,... | collective-permute-start | bytes 1572872 | tf_op jit(solution)/shard_map/ppermute | solution.py:32
  282.6 4.7 collective-permute-start.13
  288.1 4.0 collective-permute-done.12
  293.8 8.3 %collective-permute-done.13 = bf16[128,2048]{1,0:T(8,128)(2,1)S(1)} collective-permute-done((bf16[128,2048]{1,0:T(8,128)(2,1)S(1)}, bf16[128,2048]{1,0:T(8,128)(2,1)S(1)}, u32[]{:S(2)}, u32[]{:S(2)}) %collective-permute-start.13) | collective-permute-done | bytes 524320 | tf_op jit(solution)/shard_map/ppermute | solution.py:32
  303.0 10.7 %collective-permute-done.14 = bf16[128,2048]{1,0:T(8,128)(2,1)S(1)} collective-permute-done((bf16[128,2048]{1,0:T(8,128)(2,1)S(1)}, bf16[128,2048]{1,0:T(8,128)(2,1)S(1)}, u32[]{:S(2)}, u32[]{:S(2)}) %collective-permute-start.14) | collective-permute-done | bytes 524320 | tf_op jit(solution)/shard_map/ppermute | solution.py:25
  314.5 5.9 %convolution_convert_fusion = bf16[2048,256]{1,0:T(8,128)(2,1)S(1)} fusion(bf16[2048,2048]{1,0:T(8,128)(2,1)} %constant_dynamic-update-slice_fusion, bf16[1,256,2048]{2,1,0:T(8,128)(2,1)S(1)} %copy-done), kind=kOutput, calls=%fused_computation.5 | convolution fusion | flops 2148007936 | bytes 10485760 | tf_op jit(solution)/shard_map/dot_general | solution.py:79
  336.3 114.1 %all-gather.7.cloned.1.call-done = f32[256,128,128]{2,1,0:T(8,128)} async-done(((f32[16,128,128]{2,1,0:T(8,128)}), f32[256,128,128]{2,1,0:T(8,128)}) %all-gather.7.cloned.1.call-update) | async-done | bytes 16777232 | tf_op jit(solution)/shard_map/all_gather | solution.py:46
  450.5 22.7 %while.23 = (s32[]{:T(128)}, f32[16,128,128]{2,1,0:T(8,128)S(1)}, s32[]{:T(128)}, f32[16,16,128,128]{3,2,1,0:T(8,128)}, s32[]{:T(128)}, /*index=5*/s32[]{:T(128)}, s32[]{:T(128)}, s32[]{:T(128)}) while((s32[]{:T(128)}, f32[16,128,128]{2,1,0:T(8,128)S(1)}, s32[]{:T(128)}, f32[16,16,128,128]{3,2,1,0:T(8,128)}, s32[]{:T(128)}, ...), condition=%wide.region_3.4_spmd, body=%wide.region_2.3_spmd.sunk | while | flops 262150 | bytes 3145871 | solution.py:53
  473.1 3.3 fusion.1
  478.7 3.1 add_convert_fusion
  (104 shorter events, 87.1 us)
Async XLA Ops:
  7.2 137.3 %copy-start = (bf16[1,256,2048]{2,1,0:T(8,128)(2,1)S(1)}, bf16[1,256,2048]{2,1,0:T(8,128)(2,1)}, u32[]{:S(2)}) copy-start(bf16[1,256,2048]{2,1,0:T(8,128)(2,1)} %param.12) | copy-start | bytes 3145732
  7.2 134.7 %all-gather.5.cloned.1.call-start = ((), (), s32[]{:S(2)}) async-start(), calls=%async_computation.4 | async-start | bytes 17825792 | tf_op jit(solution)/shard_map/all_gather | solution.py:46
  8.8 10.1 %copy-start.1 = (bf16[1,256,2048]{1,2,0:T(8,128)(2,1)}, bf16[1,256,2048]{1,2,0:T(8,128)(2,1)S(1)}, u32[]{:S(2)}) copy-start(bf16[1,256,2048]{1,2,0:T(8,128)(2,1)S(1)} %copy.53) | copy-start | bytes 3145732
  12.1 324.1 %reduce-scatter.3.cloned.1.call-start = ((), (), s32[]{:S(2)}) async-start(), calls=%async_computation.2 | async-start | bytes 8912896 | tf_op jit(solution)/shard_map/reduce_scatter | solution.py:101
  150.1 300.2 %all-gather.7.cloned.1.call-start = ((), (), s32[]{:S(2)}) async-start(), calls=%async_computation.5 | async-start | bytes 17825792 | tf_op jit(solution)/shard_map/all_gather | solution.py:46
  159.5 29.6 %collective-permute-start = (bf16[128,2048]{1,0:T(8,128)(2,1)S(1)}, bf16[128,2048]{1,0:T(8,128)(2,1)S(1)}, u32[]{:S(2)}, u32[]{:S(2)}) collective-permute-start(bf16[128,2048]{1,0:T(8,128)(2,1)S(1)} %all_gather.15), channel_id=1, source_target_pairs={{0,2},{2,4},{4,6},{6,8},{8,10},{10,12},{12,14},{14,16},{16,18},{18... | collective-permute-start | bytes 1572872 | tf_op jit(solution)/shard_map/ppermute | solution.py:25
  160.3 29.3 %collective-permute-start.1 = (bf16[128,2048]{1,0:T(8,128)(2,1)S(1)}, bf16[128,2048]{1,0:T(8,128)(2,1)S(1)}, u32[]{:S(2)}, u32[]{:S(2)}) collective-permute-start(bf16[128,2048]{1,0:T(8,128)(2,1)S(1)} %all_gather.15), channel_id=1, source_target_pairs={{0,30},{2,0},{4,2},{6,4},{8,6},{10,8},{12,10},{14,12},{16,14},{18,... | collective-permute-start | bytes 1572872 | tf_op jit(solution)/shard_map/ppermute | solution.py:32
  189.1 12.7 %copy-start.12 = (bf16[128,2048]{1,0:T(8,128)(2,1)}, bf16[128,2048]{1,0:T(8,128)(2,1)S(1)}, u32[]{:S(2)}) copy-start(bf16[128,2048]{1,0:T(8,128)(2,1)S(1)} %collective-permute-done) | copy-start | bytes 1572868
  189.1 11.5 %collective-permute-start.2 = (bf16[128,2048]{1,0:T(8,128)(2,1)S(1)}, bf16[128,2048]{1,0:T(8,128)(2,1)}, u32[]{:S(2)}, u32[]{:S(2)}) collective-permute-start(bf16[128,2048]{1,0:T(8,128)(2,1)S(1)} %collective-permute-done), channel_id=1, source_target_pairs={{0,2},{2,4},{4,6},{6,8},{8,10},{10,12},{12,14},{14,16},{16,18},{18... | collective-permute-start | bytes 1572872 | tf_op jit(solution)/shard_map/ppermute | solution.py:25
  190.4 11.4 %collective-permute-start.3 = (bf16[128,2048]{1,0:T(8,128)(2,1)S(1)}, bf16[128,2048]{1,0:T(8,128)(2,1)}, u32[]{:S(2)}, u32[]{:S(2)}) collective-permute-start(bf16[128,2048]{1,0:T(8,128)(2,1)S(1)} %collective-permute-done.1), channel_id=1, source_target_pairs={{0,30},{2,0},{4,2},{6,4},{8,6},{10,8},{12,10},{14,12},{16,14},{18,... | collective-permute-start | bytes 1572872 | tf_op jit(solution)/shard_map/ppermute | solution.py:32
  200.6 20.5 %collective-permute-start.4 = (bf16[128,2048]{1,0:T(8,128)(2,1)}, bf16[128,2048]{1,0:T(8,128)(2,1)}, u32[]{:S(2)}, u32[]{:S(2)}) collective-permute-start(bf16[128,2048]{1,0:T(8,128)(2,1)} %collective-permute-done.2), channel_id=1, source_target_pairs={{0,2},{2,4},{4,6},{6,8},{8,10},{10,12},{12,14},{14,16},{16,18},{18... | collective-permute-start | bytes 1572872 | tf_op jit(solution)/shard_map/ppermute | solution.py:25
  201.8 26.4 %collective-permute-start.5 = (bf16[128,2048]{1,0:T(8,128)(2,1)}, bf16[128,2048]{1,0:T(8,128)(2,1)}, u32[]{:S(2)}, u32[]{:S(2)}) collective-permute-start(bf16[128,2048]{1,0:T(8,128)(2,1)} %collective-permute-done.3), channel_id=1, source_target_pairs={{0,30},{2,0},{4,2},{6,4},{8,6},{10,8},{12,10},{14,12},{16,14},{18,... | collective-permute-start | bytes 1572872 | tf_op jit(solution)/shard_map/ppermute | solution.py:32
  206.6 18.8 %copy-start.10 = (bf16[128,2048]{1,0:T(8,128)(2,1)S(1)}, bf16[128,2048]{1,0:T(8,128)(2,1)}, u32[]{:S(2)}) copy-start(bf16[128,2048]{1,0:T(8,128)(2,1)} %copy-done.9) | copy-start | bytes 1572868
  221.1 23.4 %collective-permute-start.6 = (bf16[128,2048]{1,0:T(8,128)(2,1)}, bf16[128,2048]{1,0:T(8,128)(2,1)}, u32[]{:S(2)}, u32[]{:S(2)}) collective-permute-start(bf16[128,2048]{1,0:T(8,128)(2,1)} %collective-permute-done.4), channel_id=1, source_target_pairs={{0,2},{2,4},{4,6},{6,8},{8,10},{10,12},{12,14},{14,16},{16,18},{18... | collective-permute-start | bytes 1572872 | tf_op jit(solution)/shard_map/ppermute | solution.py:25
  228.2 20.1 %collective-permute-start.7 = (bf16[128,2048]{1,0:T(8,128)(2,1)}, bf16[128,2048]{1,0:T(8,128)(2,1)S(1)}, u32[]{:S(2)}, u32[]{:S(2)}) collective-permute-start(bf16[128,2048]{1,0:T(8,128)(2,1)} %collective-permute-done.5), channel_id=1, source_target_pairs={{0,30},{2,0},{4,2},{6,4},{8,6},{10,8},{12,10},{14,12},{16,14},{18,... | collective-permute-start | bytes 1572872 | tf_op jit(solution)/shard_map/ppermute | solution.py:32
  244.5 12.9 %collective-permute-start.8 = (bf16[128,2048]{1,0:T(8,128)(2,1)}, bf16[128,2048]{1,0:T(8,128)(2,1)S(1)}, u32[]{:S(2)}, u32[]{:S(2)}) collective-permute-start(bf16[128,2048]{1,0:T(8,128)(2,1)} %collective-permute-done.6), channel_id=1, source_target_pairs={{0,2},{2,4},{4,6},{6,8},{8,10},{10,12},{12,14},{14,16},{16,18},{18... | collective-permute-start | bytes 1572872 | tf_op jit(solution)/shard_map/ppermute | solution.py:25
  248.3 12.9 %collective-permute-start.9 = (bf16[128,2048]{1,0:T(8,128)(2,1)S(1)}, bf16[128,2048]{1,0:T(8,128)(2,1)S(1)}, u32[]{:S(2)}, u32[]{:S(2)}) collective-permute-start(bf16[128,2048]{1,0:T(8,128)(2,1)S(1)} %collective-permute-done.7), channel_id=1, source_target_pairs={{0,30},{2,0},{4,2},{6,4},{8,6},{10,8},{12,10},{14,12},{16,14},{18,... | collective-permute-start | bytes 1572872 | tf_op jit(solution)/shard_map/ppermute | solution.py:32
  257.4 21.7 %collective-permute-start.10 = (bf16[128,2048]{1,0:T(8,128)(2,1)S(1)}, bf16[128,2048]{1,0:T(8,128)(2,1)S(1)}, u32[]{:S(2)}, u32[]{:S(2)}) collective-permute-start(bf16[128,2048]{1,0:T(8,128)(2,1)S(1)} %collective-permute-done.8), channel_id=1, source_target_pairs={{0,2},{2,4},{4,6},{6,8},{8,10},{10,12},{12,14},{14,16},{16,18},{18... | collective-permute-start | bytes 1572872 | tf_op jit(solution)/shard_map/ppermute | solution.py:25
  261.2 21.4 %collective-permute-start.11 = (bf16[128,2048]{1,0:T(8,128)(2,1)S(1)}, bf16[128,2048]{1,0:T(8,128)(2,1)S(1)}, u32[]{:S(2)}, u32[]{:S(2)}) collective-permute-start(bf16[128,2048]{1,0:T(8,128)(2,1)S(1)} %collective-permute-done.9), channel_id=1, source_target_pairs={{0,30},{2,0},{4,2},{6,4},{8,6},{10,8},{12,10},{14,12},{16,14},{18,... | collective-permute-start | bytes 1572872 | tf_op jit(solution)/shard_map/ppermute | solution.py:32
  279.1 13.1 %collective-permute-start.12 = (bf16[128,2048]{1,0:T(8,128)(2,1)S(1)}, bf16[128,2048]{1,0:T(8,128)(2,1)S(1)}, u32[]{:S(2)}, u32[]{:S(2)}) collective-permute-start(bf16[128,2048]{1,0:T(8,128)(2,1)S(1)} %collective-permute-done.10), channel_id=1, source_target_pairs={{0,2},{2,4},{4,6},{6,8},{8,10},{10,12},{12,14},{14,16},{16,18},{18... | collective-permute-start | bytes 1572872 | tf_op jit(solution)/shard_map/ppermute | solution.py:25
  282.6 19.5 %collective-permute-start.13 = (bf16[128,2048]{1,0:T(8,128)(2,1)S(1)}, bf16[128,2048]{1,0:T(8,128)(2,1)S(1)}, u32[]{:S(2)}, u32[]{:S(2)}) collective-permute-start(bf16[128,2048]{1,0:T(8,128)(2,1)S(1)} %collective-permute-done.11), channel_id=1, source_target_pairs={{0,30},{2,0},{4,2},{6,4},{8,6},{10,8},{12,10},{14,12},{16,14},{18,... | collective-permute-start | bytes 1572872 | tf_op jit(solution)/shard_map/ppermute | solution.py:32
  292.2 21.5 %collective-permute-start.14 = (bf16[128,2048]{1,0:T(8,128)(2,1)S(1)}, bf16[128,2048]{1,0:T(8,128)(2,1)S(1)}, u32[]{:S(2)}, u32[]{:S(2)}) collective-permute-start(bf16[128,2048]{1,0:T(8,128)(2,1)S(1)} %collective-permute-done.12), channel_id=1, source_target_pairs={{0,2},{2,4},{4,6},{6,8},{8,10},{10,12},{12,14},{14,16},{16,18},{18... | collective-permute-start | bytes 1572872 | tf_op jit(solution)/shard_map/ppermute | solution.py:25
  314.5 6.8 %copy-start.3 = (bf16[32,8,16,128]{3,2,1,0:T(8,128)(2,1)S(1)}, bf16[32,8,16,128]{3,2,1,0:T(8,128)(2,1)}, u32[]{:S(2)}) copy-start(bf16[32,8,16,128]{3,2,1,0:T(8,128)(2,1)} %copy-done.2) | copy-start | bytes 3145732
  325.4 158.7 %reduce-scatter.5.cloned.1.call-start = ((), (), s32[]{:S(2)}) async-start(), calls=%async_computation.3 | async-start | bytes 786432 | tf_op jit(solution)/shard_map/reduce_scatter | solution.py:112
  (8 other events, 18.7 us)
Sparse Core Ops, SparseCore 0:
  12.2 129.5 all-gather.4
  150.2 158.7 reduce-scatter.2
  325.5 124.7 all-gather.6
  452.5 12.6 reduce-scatter.4
